TPU v7x, 512 devices: a whole 4x4x16 slice. The times are simulated.
512 devices in a mesh: exp: 64 (over x, z), rep: 8 (over y, core).
Axes of the slice: x: 4, y: 4, z: 16, core: 2. Of those that a mesh axis runs over, the one named last changes fastest.
Arguments:
- latent: bfloat16 [128, 16, 64], P('exp'), may hold values from -6 to 6
- stem_weight: bfloat16 [144, 1536], replicated, may hold values from -0.5 to 0.5
- norm_gain: float32 [1536], replicated, may hold values from 0.4 to 1.6
- router_weight: bfloat16 [1536, 8], replicated, may hold values from -0.15625 to 0.15625
- routes: int32 [8192, 2], P('exp'), may hold values from 0 to 7, all different within a row; in each aligned block of 128 rows (0 to 127, 128 to 255, ...) at most 40 rows name the same one
- gate_weight: bfloat16 [1536, 24576], P('rep', 'exp'), may hold values from -0.15625 to 0.15625
- up_weight: bfloat16 [1536, 24576], P('rep', 'exp'), may hold values from -0.15625 to 0.15625
- down_weight: bfloat16 [24576, 1536], P('exp', 'rep'), may hold values from -0.109375 to 0.109375
- grad_mixed: bfloat16 [8192, 1536], P('exp'), may hold values from -6 to 6
Outputs:
- mixed: bfloat16 [8192, 1536], P('exp')
- grad_latent: float32 [128, 16, 64], P('exp')
- grad_gate: float32 [1536, 24576], P('rep', 'exp')
- grad_up: float32 [1536, 24576], P('rep', 'exp')
- grad_down: float32 [24576, 1536], P('exp', 'rep')
Inputs may be any that keep to these rules, and one draw needn't show every extreme that they name: `routes`: A token's 2 experts differ. Within the 128 tokens of one device, no expert is named more than 40 times, and in every draw some device's tokens name some expert exactly 40 times.
All inputs are finite; a program needn't handle non-finite values.
Results may differ from a plain program's by a relative error of at most 0.023.
Values may be sent and summed in bfloat16 or wider, within the bound.
A program may use at most 64 MiB of HBM per device.

v0:
```python
import jax
import jax.numpy as jnp
from jax import lax
from jax.sharding import PartitionSpec as P

CAP = 40
F32 = jnp.float32
BF = jnp.bfloat16


def dot32(a, b, dims=None):
    if dims is None:
        return jnp.dot(a, b, preferred_element_type=F32)
    return lax.dot_general(a, b, (dims, ((), ())), preferred_element_type=F32)


def split(v):
    hi = v.astype(BF)
    return (hi, (v - hi.astype(F32)).astype(BF))


def halo(cells):
    count = lax.axis_size("exp")
    head, tail = (cells[:1], cells[-1:])
    return jnp.concatenate(
        [
            lax.ppermute(tail, "exp", [(i, i + 1) for i in range(count - 1)]),
            cells,
            lax.ppermute(head, "exp", [(i + 1, i) for i in range(count - 1)]),
        ],
        axis=0,
    )


def gating(picked):
    chosen = jax.nn.sigmoid(picked)
    return chosen / jnp.sum(chosen, axis=-1, keepdims=True)


def local(
    latent,
    stem_weight,
    norm_gain,
    router_weight,
    routes,
    gate_weight,
    up_weight,
    down_weight,
    grad_mixed,
):
    rows_here, channels, width = latent.shape
    taps, model_width = stem_weight.shape
    experts = router_weight.shape[1]
    top = routes.shape[1]
    tok = rows_here * width
    nrep = lax.axis_size("rep")
    nexp = lax.axis_size("exp")
    shards = nexp // experts
    sub = CAP // nrep
    rep = lax.axis_index("rep")
    across = [[e * shards + m for e in range(experts)] for m in range(shards)]
    along = [[e * shards + m for m in range(shards)] for e in range(experts)]
    dsl = model_width // nrep
    s_here = lax.dynamic_slice_in_dim(stem_weight, rep * dsl, dsl, 1)
    gain_here = lax.dynamic_slice_in_dim(norm_gain, rep * dsl, dsl, 0)
    sg_hi, sg_lo = split(s_here.astype(F32) * gain_here)
    w2 = jnp.concatenate([gate_weight, up_weight], axis=1)
    g_full = lax.psum(dot32(sg_hi, w2) + dot32(sg_lo, w2), "rep")
    g_hi, g_lo = split(g_full)
    down = lax.all_gather(down_weight, "rep", axis=1, tiled=True)
    padded = jnp.pad(halo(latent), ((0, 0), (0, 0), (1, 1)))
    pieces = jnp.stack(
        [padded[i : i + rows_here, :, j : j + width] for i in range(3) for j in range(3)], axis=0
    )
    patches = jnp.transpose(pieces, (1, 3, 0, 2)).reshape(tok, taps)
    stem = dot32(patches, stem_weight).astype(BF)
    sv = stem.astype(F32)
    rstd = lax.rsqrt(jnp.mean(sv * sv, axis=-1, keepdims=True) + 1e-06)
    normed = (sv * rstd * norm_gain).astype(BF)
    logits = dot32(normed, router_weight)
    selector = (routes[:, :, None] == jnp.arange(experts, dtype=jnp.int32)).astype(F32)
    picked = jnp.sum(logits[:, None, :] * selector, axis=-1)
    gates = gating(picked)
    sel_i = selector.astype(jnp.int32)
    both = jnp.sum(sel_i, axis=1)
    before = jnp.cumsum(both, axis=0) - both
    position = jnp.sum(sel_i * before[:, None, :], axis=-1)
    slot = routes * CAP + position
    slot_ids = jnp.arange(experts * CAP, dtype=jnp.int32)
    hot = [slot[:, k][:, None] == slot_ids[None, :] for k in range(top)]
    hot_here = [
        lax.dynamic_slice_in_dim(h.reshape(tok, experts, CAP), rep * sub, sub, 2).reshape(
            tok, experts * sub
        )
        for h in hot
    ]
    hot_any = sum((h.astype(BF) for h in hot_here))
    rstd_parts = split(rstd)
    gate_parts = [split(gates[:, k][:, None]) for k in range(top)]
    wide = jnp.concatenate(
        [grad_mixed, patches, rstd_parts[0], rstd_parts[1], jnp.zeros((tok, 110), BF)], axis=1
    )
    send = dot32(hot_any, wide, ((0,), (0,))).astype(BF)
    send_gate = sum(
        (
            dot32(hot_here[k].astype(BF), jnp.concatenate(gate_parts[k], axis=1), ((0,), (0,)))
            for k in range(top)
        )
    ).astype(BF)
    send = jnp.concatenate(
        [send[:, : model_width + 146], send_gate, send[:, model_width + 148 :]], axis=1
    )
    send = send.reshape(experts, sub, -1)
    stage = lax.all_to_all(
        send, "exp", split_axis=0, concat_axis=0, tiled=True, axis_index_groups=across
    )
    recv = lax.all_gather(stage, "exp", axis=0, tiled=True, axis_index_groups=along)
    flat = recv.reshape(-1, recv.shape[-1])
    gm = flat[:, :model_width]
    pr = flat[:, model_width : model_width + taps]
    extra = flat[:, model_width + taps : model_width + taps + 4].astype(F32)
    rs = extra[:, 0:1] + extra[:, 1:2]
    gt = extra[:, 2:3] + extra[:, 3:4]
    hid = gate_weight.shape[1]
    pre = rs * (dot32(pr, g_hi) + dot32(pr, g_lo))
    pg, pu = (pre[:, :hid], pre[:, hid:])
    sigma = jax.nn.sigmoid(pg)
    hidden = pg * sigma * pu
    hg = (gt * hidden).astype(BF)
    out = dot32(hg, down)
    u = dot32(gm, down, ((1,), (1,)))
    gg = jnp.sum(hidden * u, axis=-1, keepdims=True)
    gu = rs * gt * u
    dpre = jnp.concatenate(
        [gu * pu * sigma * (1.0 + pg * (1.0 - sigma)), gu * pg * sigma], axis=1
    ).astype(BF)
    back = dot32(dpre, g_hi, ((1,), (1,))) + dot32(dpre, g_lo, ((1,), (1,)))
    t_part = dot32(pr, dpre, ((0,), (0,)))
    d_part = dot32(gm, hg, ((0,), (0,)))
    gg_hi, gg_lo = split(gg)
    ret = jnp.concatenate(
        [out.astype(BF), back.astype(BF), gg_hi, gg_lo, jnp.zeros((out.shape[0], 110), BF)], axis=1
    ).reshape(shards, experts, sub, -1)
    summed = lax.psum_scatter(ret, "exp", scatter_dimension=0, axis_index_groups=along, tiled=True)[
        0
    ]
    mine = lax.all_to_all(
        summed, "exp", split_axis=0, concat_axis=0, tiled=True, axis_index_groups=across
    )
    slots_back = lax.all_gather(mine, "rep", axis=1, tiled=True).reshape(experts * CAP, -1)
    t_full = lax.psum(t_part, "rep")
    t_hi, t_lo = split(t_full)
    gw = (dot32(s_here, t_hi, ((0,), (0,))) + dot32(s_here, t_lo, ((0,), (0,)))) * gain_here[
        :, None
    ]
    grad_gate, grad_up = (gw[:, :hid], gw[:, hid:])
    grad_down = (
        lax.psum_scatter(d_part.astype(BF), "rep", scatter_dimension=0, tiled=True).astype(F32).T
    )
    hot_sum = sum((h.astype(BF) for h in hot))
    tok_sum = dot32(hot_sum, slots_back)
    mixed = (sv + tok_sum[:, :model_width]).astype(BF)
    ggs = slots_back[:, model_width + taps : model_width + taps + 2]
    grad_gates = jnp.concatenate(
        [jnp.sum(dot32(hot[k].astype(BF), ggs), axis=-1, keepdims=True) for k in range(top)], axis=1
    )
    _, gate_pull = jax.vjp(gating, picked)
    grad_picked = gate_pull(grad_gates)[0]
    grad_logits = jnp.sum(selector * grad_picked[:, :, None], axis=1)
    sg_all = stem_weight.astype(F32) * norm_gain
    rproj = jnp.dot(sg_all, router_weight.astype(F32), precision=lax.Precision.HIGHEST)
    b = tok_sum[:, model_width : model_width + taps] + rstd * jnp.dot(
        grad_logits, rproj.T, precision=lax.Precision.HIGHEST
    )
    c = jnp.sum(patches.astype(F32) * b, axis=-1, keepdims=True) * (rstd * rstd / model_width)
    proj = (
        dot32(grad_mixed, stem_weight, ((1,), (1,)))
        + b
        - c * dot32(stem, stem_weight, ((1,), (1,)))
    )
    block = halo(proj.reshape(rows_here, width, taps)).reshape(rows_here + 2, width, 9, channels)
    shifted = jnp.pad(block, ((0, 0), (1, 1), (0, 0), (0, 0)))
    terms = [
        shifted[2 - i : 2 - i + rows_here, 2 - j : 2 - j + width, 3 * i + j, :]
        for i in range(3)
        for j in range(3)
    ]
    grad_latent = sum(terms).transpose(0, 2, 1)
    return (mixed, grad_latent, grad_gate, grad_up, grad_down)


def solution(mesh):
    return jax.shard_map(
        local,
        mesh=mesh,
        in_specs=(
            P("exp", None, None),
            P(),
            P(),
            P(),
            P("exp", None),
            P("rep", "exp"),
            P("rep", "exp"),
            P("exp", "rep"),
            P("exp", None),
        ),
        out_specs=(
            P("exp", None),
            P("exp", None, None),
            P("rep", "exp"),
            P("rep", "exp"),
            P("exp", "rep"),
        ),
        check_vma=False,
    )
```

profile of v0, /device:TPU:96, one launch (start us, length us, event | category | flops | bytes accessed | tf_op | source)
XLA Modules:
  0.0 310.6 jit_solution(7389787148921936075)
XLA Ops:
  8.8 5.0 %collective-permute-start = (bf16[1,16,64]{2,1,0:T(8,128)(2,1)S(1)}, bf16[1,16,64]{2,1,0:T(8,128)(2,1)S(1)}, u32[]{:S(2)}, u32[]{:S(2)}) collective-permute-start(bf16[1,16,64]{2,1,0:T(8,128)(2,1)S(1)} %get-tuple-element.47), channel_id=1, source_target_pairs={{0,8},{8,16},{16,24},{24,32},{32,40},{40,48},{48,56},{56,64},{64,7... | collective-permute-start | bytes 6152 | tf_op jit(solution)/shard_map/ppermute | solution.py:27
  13.9 1.9 collective-permute-start.1
  18.5 2.1 collective-permute-done.1
  26.1 31.8 %all_to_all.10 = bf16[8,5,1792]{2,1,0:T(8,128)(2,1)S(1)} all-to-all(bf16[8,5,1792]{2,1,0:T(8,128)(2,1)S(1)} %reshape.239), channel_id=1, replica_groups={{0,64,128,192,256,320,384,448},{8,72,136,200,264,328,392,456},{16,80,14..., dimensions={0} | all-to-all | bytes 286720 | tf_op jit(solution)/shard_map/all_to_all | solution.py:114
  59.1 1.1 convolution_add_fusion.2
  61.0 46.7 %all-gather.4.cloned.1.call-done = bf16[64,5,1792]{2,0,1:T(8,128)(2,1)} async-done(((bf16[8,5,1792]{2,0,1:T(8,128)(2,1)}), bf16[64,5,1792]{2,0,1:T(8,128)(2,1)}) %all-gather.4.cloned.1.call-update) | async-done | bytes 1146896 | tf_op jit(solution)/shard_map/all_gather | solution.py:117
  107.7 1.9 copy.150
  109.6 1.3 reshape.240
  110.9 1.0 slice_convert_fusion
  112.3 23.1 %all-reduce.5.cloned.1.call-done = f32[144,768]{1,0:T(8,128)} async-done(((f32[144,768]{1,0:T(8,128)}), f32[144,768]{1,0:T(8,128)}) %all-reduce.5.cloned.1.call-update) | async-done | bytes 442384 | tf_op jit(solution)/shard_map/psum | solution.py:68
  135.4 1.4 fusion.29
  136.9 1.2 fusion
  138.1 11.5 %all-gather.6.cloned.1.call-done = bf16[384,1536]{0,1:T(8,128)(2,1)} async-done(((bf16[384,192]{0,1:T(8,128)(2,1)}), bf16[384,1536]{0,1:T(8,128)(2,1)}) %all-gather.6.cloned.1.call-update) | async-done | bytes 1179664 | tf_op jit(solution)/shard_map/all_gather | solution.py:70
  149.6 3.2 %multiply_convert_fusion.1 = (bf16[320,384]{1,0:T(8,128)(2,1)S(1)}, bf16[320,384]{1,0:T(8,128)(2,1)S(1)}, f32[320]{0:T(512)S(1)}, f32[320,384]{1,0:T(8,128)}) fusion(f32[320,768]{1,0:T(8,128)} %fusion, f32[320]{0:T(512)S(1)} %get-tuple-element.30, bf16[384,1536]{0,1:T(8,128)(2,1)} %all-gather.6.cloned.1.call-done, bf16[320,1792]{1,0:T(8,128)(2,1)S(1)} %copy-done.3), kind=kOutput, calls=%fused_computation.36 | convolution fusion | flops 379698880 | bytes 4132096 | tf_op jit(solution)/shard_map/dot_general | solution.py:14
  153.0 1.0 copy.155
  154.0 1.0 copy.154
  156.6 2.0 convolution_convert_fusion.1
  159.1 3.5 %concatenate.74 = bf16[8,8,5,1792]{3,2,1,0:T(8,128)(2,1)} concatenate(bf16[8,8,5,1536]{3,2,1,0:T(8,128)(2,1)S(1)} %concatenate.71, bf16[8,8,5,144]{3,2,1,0:T(8,128)(2,1)} %concatenate.73, bf16[8,8,5,1]{3,2,1,0:T(8,128)(2,1)} %copy.154, bf16[8,8,5,1]{3,2,1,0:T(8,128)(2,1)} %copy.155, bf16[8,8,5,110]{3,2,1,0:T(8,128)(2,1)S(1)} %broadcast_in_dim.9), dimensions={3} | concatenate | bytes 2293760 | tf_op jit(solution)/shard_map/concatenate | solution.py:141
  162.7 1.2 copy-done.4
  164.0 1.1 fusion.25
  165.1 2.0 convolution_convert_fusion
  167.2 53.7 %reduce-scatter.3.cloned.1.call-done = bf16[1,8,5,1792]{3,2,1,0:T(8,128)(2,1)} async-done(((bf16[8,8,5,1792]{3,2,1,0:T(8,128)(2,1)}), bf16[1,8,5,1792]{3,2,1,0:T(8,128)(2,1)}) %reduce-scatter.3.cloned.1.call-update) | async-done | bytes 143376 | tf_op jit(solution)/shard_map/reduce_scatter | solution.py:144
  220.9 29.1 %all_to_all.11 = bf16[8,5,1792]{2,1,0:T(8,128)(2,1)S(1)} all-to-all(bf16[8,5,1792]{2,1,0:T(8,128)(2,1)} %bitcast.103), channel_id=1, replica_groups={{0,64,128,192,256,320,384,448},{8,72,136,200,264,328,392,456},{16,80,14..., dimensions={0} | all-to-all | bytes 286720 | tf_op jit(solution)/shard_map/all_to_all | solution.py:147
  251.3 1.4 fusion.32
  253.1 0.9 fusion.84
  253.9 18.8 %reduce-scatter.5.cloned.1.call-done = bf16[192,384]{1,0:T(8,128)(2,1)} async-done(((bf16[1536,384]{1,0:T(8,128)(2,1)}), bf16[192,384]{1,0:T(8,128)(2,1)}) %reduce-scatter.5.cloned.1.call-update) | async-done | bytes 147472 | tf_op jit(solution)/shard_map/reduce_scatter | solution.py:158
  272.7 1.7 convert_bitcast_fusion
  274.4 11.9 %all-gather.8.cloned.1.call-done = bf16[8,40,1792]{2,0,1:T(8,128)(2,1)} async-done(((bf16[8,5,1792]{2,0,1:T(8,128)(2,1)}), bf16[8,40,1792]{2,0,1:T(8,128)(2,1)}) %all-gather.8.cloned.1.call-update) | async-done | bytes 1146896 | tf_op jit(solution)/shard_map/all_gather | solution.py:150
  286.3 1.4 copy.157
  289.9 4.7 %collective-permute-start.2 = (f32[1,64,144]{1,2,0:T(8,128)S(1)}, f32[1,64,144]{1,2,0:T(8,128)S(1)}, u32[]{:S(2)}, u32[]{:S(2)}) collective-permute-start(f32[1,64,144]{1,2,0:T(8,128)S(1)} %get-tuple-element.45), channel_id=1, source_target_pairs={{0,8},{8,16},{16,24},{24,32},{32,40},{40,48},{48,56},{56,64},{64,7... | collective-permute-start | bytes 110600 | tf_op jit(solution)/shard_map/ppermute | solution.py:27
  294.6 1.9 collective-permute-start.3
  297.5 4.6 %collective-permute-done.3 = f32[1,64,144]{1,2,0:T(8,128)S(1)} collective-permute-done((f32[1,64,144]{1,2,0:T(8,128)S(1)}, f32[1,64,144]{1,2,0:T(8,128)S(1)}, u32[]{:S(2)}, u32[]{:S(2)}) %collective-permute-start.3) | collective-permute-done | bytes 36896 | tf_op jit(solution)/shard_map/ppermute | solution.py:29
  (137 shorter events, 19.8 us)
Async XLA Ops:
  8.0 16.5 %copy-start = (bf16[1536,8]{0,1:T(8,128)(2,1)S(1)}, bf16[1536,8]{0,1:T(8,128)(2,1)}, u32[]{:S(2)}) copy-start(bf16[1536,8]{0,1:T(8,128)(2,1)} %param.12) | copy-start | bytes 73732
  8.0 16.1 %copy-start.1 = (bf16[144,1536]{1,0:T(8,128)(2,1)S(1)}, bf16[144,1536]{1,0:T(8,128)(2,1)}, u32[]{:S(2)}) copy-start(bf16[144,1536]{1,0:T(8,128)(2,1)} %param.10) | copy-start | bytes 1327108
  8.0 16.5 %copy-start.17 = (f32[1536]{0:T(1024)S(1)}, f32[1536]{0:T(1024)}, u32[]{:S(2)}) copy-start(f32[1536]{0:T(1024)} %param.11) | copy-start | bytes 18436
  8.0 99.6 %all-gather.4.cloned.1.call-start = ((), (), s32[]{:S(2)}) async-start(), calls=%async_computation.4 | async-start | bytes 1290240 | tf_op jit(solution)/shard_map/all_gather | solution.py:117
  8.8 9.6 %collective-permute-start = (bf16[1,16,64]{2,1,0:T(8,128)(2,1)S(1)}, bf16[1,16,64]{2,1,0:T(8,128)(2,1)S(1)}, u32[]{:S(2)}, u32[]{:S(2)}) collective-permute-start(bf16[1,16,64]{2,1,0:T(8,128)(2,1)S(1)} %get-tuple-element.47), channel_id=1, source_target_pairs={{0,8},{8,16},{16,24},{24,32},{32,40},{40,48},{48,56},{56,64},{64,7... | collective-permute-start | bytes 6152 | tf_op jit(solution)/shard_map/ppermute | solution.py:27
  13.9 6.7 %collective-permute-start.1 = (bf16[1,16,64]{2,1,0:T(8,128)(2,1)S(1)}, bf16[1,16,64]{2,1,0:T(8,128)(2,1)S(1)}, u32[]{:S(2)}, u32[]{:S(2)}) collective-permute-start(bf16[1,16,64]{2,1,0:T(8,128)(2,1)S(1)} %get-tuple-element.48), channel_id=1, source_target_pairs={{8,0},{16,8},{24,16},{32,24},{40,32},{48,40},{56,48},{64,56},{72,6... | collective-permute-start | bytes 6152 | tf_op jit(solution)/shard_map/ppermute | solution.py:29
  16.8 8.0 %copy-start.16 = (s32[128,2]{0,1:T(2,128)S(1)}, s32[128,2]{0,1:T(2,128)}, u32[]{:S(2)}) copy-start(s32[128,2]{0,1:T(2,128)} %param.13) | copy-start | bytes 3076
  21.4 4.2 %copy-start.6 = (bf16[128,1536]{1,0:T(8,128)(2,1)S(1)}, bf16[128,1536]{1,0:T(8,128)(2,1)}, u32[]{:S(2)}) copy-start(bf16[128,1536]{1,0:T(8,128)(2,1)} %param.17) | copy-start | bytes 1179652
  25.7 33.1 %copy-start.14 = (bf16[192,384]{1,0:T(8,128)(2,1)S(1)}, bf16[192,384]{1,0:T(8,128)(2,1)}, u32[]{:S(2)}) copy-start(bf16[192,384]{1,0:T(8,128)(2,1)} %param.14) | copy-start | bytes 442372
  25.7 33.1 %copy-start.15 = (bf16[192,384]{1,0:T(8,128)(2,1)S(1)}, bf16[192,384]{1,0:T(8,128)(2,1)}, u32[]{:S(2)}) copy-start(bf16[192,384]{1,0:T(8,128)(2,1)} %param.15) | copy-start | bytes 442372
  58.6 76.8 %all-reduce.5.cloned.1.call-start = ((), (), s32[]{:S(2)}) async-start(), calls=%async_computation.5 | async-start | bytes 884736 | tf_op jit(solution)/shard_map/psum | solution.py:68
  60.2 89.4 %all-gather.6.cloned.1.call-start = ((), (), s32[]{:S(2)}) async-start(), calls=%async_computation.6 | async-start | bytes 1327104 | tf_op jit(solution)/shard_map/all_gather | solution.py:70
  61.0 159.9 %reduce-scatter.3.cloned.1.call-start = ((), (), s32[]{:S(2)}) async-start(), calls=%async_computation.7 | async-start | bytes 2064384 | tf_op jit(solution)/shard_map/reduce_scatter | solution.py:144
  111.9 25.0 %copy-start.3 = (bf16[320,1792]{1,0:T(8,128)(2,1)S(1)}, bf16[320,1792]{1,0:T(8,128)(2,1)}, u32[]{:S(2)}) copy-start(bf16[320,1792]{1,0:T(8,128)(2,1)} %reshape.240) | copy-start | bytes 3440644
  135.4 1.4 copy-start.2
  152.7 2.9 copy-start.8
  152.7 3.0 copy-start.10
  155.3 1.3 copy-start.12
  162.6 1.3 copy-start.4
  162.6 1.3 copy-start.9
  162.6 1.4 copy-start.11
  162.6 2.5 copy-start.13
  162.7 88.6 %all-reduce.7.cloned.1.call-start = ((), (), s32[]{:S(2)}) async-start(), calls=%async_computation.9 | async-start | bytes 884736 | tf_op jit(solution)/shard_map/psum | solution.py:151
  165.1 107.6 %reduce-scatter.5.cloned.1.call-start = ((), (), s32[]{:S(2)}) async-start(), calls=%async_computation.10 | async-start | bytes 1327104 | tf_op jit(solution)/shard_map/reduce_scatter | solution.py:158
  167.2 119.1 %all-gather.8.cloned.1.call-start = ((), (), s32[]{:S(2)}) async-start(), calls=%async_computation.8 | async-start | bytes 1290240 | tf_op jit(solution)/shard_map/all_gather | solution.py:150
  251.3 1.4 copy-start.5
  288.2 1.0 copy-start.7
  289.9 7.6 %collective-permute-start.2 = (f32[1,64,144]{1,2,0:T(8,128)S(1)}, f32[1,64,144]{1,2,0:T(8,128)S(1)}, u32[]{:S(2)}, u32[]{:S(2)}) collective-permute-start(f32[1,64,144]{1,2,0:T(8,128)S(1)} %get-tuple-element.45), channel_id=1, source_target_pairs={{0,8},{8,16},{16,24},{24,32},{32,40},{40,48},{48,56},{56,64},{64,7... | collective-permute-start | bytes 110600 | tf_op jit(solution)/shard_map/ppermute | solution.py:27
  294.6 7.5 %collective-permute-start.3 = (f32[1,64,144]{1,2,0:T(8,128)S(1)}, f32[1,64,144]{1,2,0:T(8,128)S(1)}, u32[]{:S(2)}, u32[]{:S(2)}) collective-permute-start(f32[1,64,144]{1,2,0:T(8,128)S(1)} %get-tuple-element.46), channel_id=1, source_target_pairs={{8,0},{16,8},{24,16},{32,24},{40,32},{48,40},{56,48},{64,56},{72,6... | collective-permute-start | bytes 110600 | tf_op jit(solution)/shard_map/ppermute | solution.py:29
Sparse Core Ops, SparseCore 0:
  58.7 48.8 all-gather.3
  109.8 39.7 all-gather.5
  162.8 58.0 reduce-scatter.2
  223.6 49.1 reduce-scatter.4
Sparse Core Ops, SparseCore 1:
  61.5 73.9 all-reduce.4
  165.5 77.1 all-reduce.6
  250.8 35.4 all-gather.7
where the time goes:
time: 312 us; the launch traced here: 311 us
  waiting for transfers between devices  173 us (55%)
  blocking collectives  60.9 us (20%)
  local copies, waits for them, and re-layouts  19.4 us (6%)
  matrix products  18.2 us (6%)
  between operations  16 us (5%)
  starting transfers between devices  13.8 us (4%)
  other arithmetic  9.23 us (3%)
    reduce_scatter x1, waiting for transfers between devices, local(): lax.psum_scatter(ret, 'exp', scatter_dimension=0, axis_index_groups=along...  53.7 us
    all_gather x1, waiting for transfers between devices, local(): lax.all_gather(stage, 'exp', axis=0, tiled=True, axis_index_groups=along)  46.7 us
    all_to_all x1, blocking collectives, local(): lax.all_to_all(send, 'exp', split_axis=0, concat_axis=0, tiled=True, axis...  31.8 us
    all_to_all x1, blocking collectives, local(): lax.all_to_all(summed, 'exp', split_axis=0, concat_axis=0, tiled=True, ax...  29.1 us
    psum x1, waiting for transfers between devices, local(): g_full = lax.psum(dot32(sg_hi, w2) + dot32(sg_lo, w2), 'rep')  23.1 us
    reduce_scatter x1, waiting for transfers between devices, local(): lax.psum_scatter(d_part.astype(BF), 'rep', scatter_dimension=0, tiled=True)  18.8 us
    all_gather x1, waiting for transfers between devices, local(): lax.all_gather(mine, 'rep', axis=1, tiled=True).reshape(experts * CAP, -1)  11.9 us
    all_gather x1, waiting for transfers between devices, local(): down = lax.all_gather(down_weight, 'rep', axis=1, tiled=True)  11.5 us
  transfers between devices with their start and end apart: 11, of which 8 were waited for; matrix products, arithmetic and copies ran while one was open for 7% of the time, Pallas kernels for 0%

commit v1 on v0

--- a/solution.py
+++ b/solution.py
@@ -65,7 +65,7 @@
     gain_here = lax.dynamic_slice_in_dim(norm_gain, rep * dsl, dsl, 0)
     sg_hi, sg_lo = split(s_here.astype(F32) * gain_here)
     w2 = jnp.concatenate([gate_weight, up_weight], axis=1)
-    g_full = lax.psum(dot32(sg_hi, w2) + dot32(sg_lo, w2), "rep")
+    g_full = jnp.sum(lax.all_gather(dot32(sg_hi, w2) + dot32(sg_lo, w2), "rep"), axis=0)
     g_hi, g_lo = split(g_full)
     down = lax.all_gather(down_weight, "rep", axis=1, tiled=True)
     padded = jnp.pad(halo(latent), ((0, 0), (0, 0), (1, 1)))

time: 312 us -> 444 us (1.42)
  waiting for transfers between devices: 173 us -> 310 us
    psum x1, waiting for transfers between devices: 0.03 us -> 57.5 us  [local(): t_full = lax.psum(t_part, 'rep')]
    all_gather x0 -> x1, waiting for transfers between devices: none -> 44.2 us  [local(): lax.all_gather(dot32(sg_hi, w2) + dot32(sg_lo, w2), 'rep')]
    psum x1 -> x0, waiting for transfers between devices: 23.1 us -> none  [local(): g_full = lax.psum(dot32(sg_hi, w2) + dot32(sg_lo, w2), 'rep')]
    reduce_scatter x1, waiting for transfers between devices: 18.8 us -> 39.1 us  [local(): lax.psum_scatter(d_part.astype(BF), 'rep', scatter_dimension=0, tiled=True)]
    all_gather x1, waiting for transfers between devices: 11.5 us -> 30.4 us  [local(): down = lax.all_gather(down_weight, 'rep', axis=1, tiled=True)]
    all_gather x1, waiting for transfers between devices: 11.9 us -> 30.5 us  [local(): lax.all_gather(mine, 'rep', axis=1, tiled=True).reshape(experts * CAP, -1)]
  transfers between devices with their start and end apart: 11 -> 11, of which waited for: 8 -> 9; matrix products, arithmetic and copies ran while one was open for 7% -> 4% of each run, Pallas kernels for 0% -> 0%
where the time goes in v1:
time: 444 us
  waiting for transfers between devices  310 us (70%)
  blocking collectives  60.4 us (14%)
  local copies, waits for them, and re-layouts  17 us (4%)
  matrix products  16.4 us (4%)
  between operations  14.8 us (3%)
  starting transfers between devices  13.8 us (3%)
  other arithmetic  11.1 us (2%)
    psum x1, waiting for transfers between devices, local(): t_full = lax.psum(t_part, 'rep')  57.5 us
    reduce_scatter x1, waiting for transfers between devices, local(): lax.psum_scatter(ret, 'exp', scatter_dimension=0, axis_index_groups=along...  53.9 us
    all_gather x1, waiting for transfers between devices, local(): lax.all_gather(stage, 'exp', axis=0, tiled=True, axis_index_groups=along)  46.8 us
    all_gather x1, waiting for transfers between devices, local(): lax.all_gather(dot32(sg_hi, w2) + dot32(sg_lo, w2), 'rep')  44.2 us
    reduce_scatter x1, waiting for transfers between devices, local(): lax.psum_scatter(d_part.astype(BF), 'rep', scatter_dimension=0, tiled=True)  39.1 us
    all_to_all x1, blocking collectives, local(): lax.all_to_all(send, 'exp', split_axis=0, concat_axis=0, tiled=True, axis...  31.8 us
    all_gather x1, waiting for transfers between devices, local(): lax.all_gather(mine, 'rep', axis=1, tiled=True).reshape(experts * CAP, -1)  30.5 us
    all_gather x1, waiting for transfers between devices, local(): down = lax.all_gather(down_weight, 'rep', axis=1, tiled=True)  30.4 us
  transfers between devices with their start and end apart: 11, of which 9 were waited for; matrix products, arithmetic and copies ran while one was open for 4% of the time, Pallas kernels for 0%

profile of v1, /device:TPU:96, one launch (start us, length us, event | category | flops | bytes accessed | tf_op | source)
XLA Modules:
  0.0 443.5 jit_solution(16337189508034964792)
XLA Ops:
  8.0 5.0 %collective-permute-start = (bf16[1,16,64]{2,1,0:T(8,128)(2,1)S(1)}, bf16[1,16,64]{2,1,0:T(8,128)(2,1)S(1)}, u32[]{:S(2)}, u32[]{:S(2)}) collective-permute-start(bf16[1,16,64]{2,1,0:T(8,128)(2,1)S(1)} %get-tuple-element.47), channel_id=1, source_target_pairs={{0,8},{8,16},{16,24},{24,32},{32,40},{40,48},{48,56},{56,64},{64,7... | collective-permute-start | bytes 6152 | tf_op jit(solution)/shard_map/ppermute | solution.py:27
  13.0 1.9 collective-permute-start.1
  17.7 2.1 collective-permute-done.1
  19.7 0.8 fusion.59
  26.0 31.8 %all_to_all.10 = bf16[8,5,1792]{2,1,0:T(8,128)(2,1)S(1)} all-to-all(bf16[8,5,1792]{2,1,0:T(8,128)(2,1)S(1)} %reshape.239), channel_id=1, replica_groups={{0,64,128,192,256,320,384,448},{8,72,136,200,264,328,392,456},{16,80,14..., dimensions={0} | all-to-all | bytes 286720 | tf_op jit(solution)/shard_map/all_to_all | solution.py:114
  58.9 1.1 convolution_add_fusion.2
  60.8 46.8 %all-gather.6.cloned.1.call-done = bf16[64,5,1792]{2,0,1:T(8,128)(2,1)} async-done(((bf16[8,5,1792]{2,0,1:T(8,128)(2,1)}), bf16[64,5,1792]{2,0,1:T(8,128)(2,1)}) %all-gather.6.cloned.1.call-update) | async-done | bytes 1146896 | tf_op jit(solution)/shard_map/all_gather | solution.py:117
  107.6 1.9 copy.150
  110.2 0.9 multiply_reduce_fusion.1
  111.0 44.2 %all-gather.12.cloned.1.call-done = f32[1152,768]{1,0:T(8,128)} async-done(((f32[144,768]{1,0:T(8,128)}), f32[1152,768]{1,0:T(8,128)}) %all-gather.12.cloned.1.call-update) | async-done | bytes 3538960 | tf_op jit(solution)/shard_map/all_gather | solution.py:68
  155.3 2.3 reduce_sum.123
  158.1 30.4 %all-gather.8.cloned.1.call-done = bf16[384,1536]{0,1:T(8,128)(2,1)} async-done(((bf16[384,192]{0,1:T(8,128)(2,1)}), bf16[384,1536]{0,1:T(8,128)(2,1)}) %all-gather.8.cloned.1.call-update) | async-done | bytes 1179664 | tf_op jit(solution)/shard_map/all_gather | solution.py:70
  188.5 3.5 multiply_convert_fusion.1
  193.4 2.0 convolution_convert_fusion.1
  195.8 0.8 reduce_sum.125
  197.5 2.1 concatenate.74
  199.7 1.2 copy-done.5
  200.9 1.1 fusion.25
  202.0 2.0 convolution_convert_fusion
  204.1 53.9 %reduce-scatter.3.cloned.1.call-done = bf16[1,8,5,1792]{3,2,1,0:T(8,128)(2,1)} async-done(((bf16[8,8,5,1792]{3,2,1,0:T(8,128)(2,1)}), bf16[1,8,5,1792]{3,2,1,0:T(8,128)(2,1)}) %reduce-scatter.3.cloned.1.call-update) | async-done | bytes 143376 | tf_op jit(solution)/shard_map/reduce_scatter | solution.py:144
  258.1 28.7 %all_to_all.11 = bf16[8,5,1792]{2,1,0:T(8,128)(2,1)S(1)} all-to-all(bf16[8,5,1792]{2,1,0:T(8,128)(2,1)} %bitcast.105), channel_id=1, replica_groups={{0,64,128,192,256,320,384,448},{8,72,136,200,264,328,392,456},{16,80,14..., dimensions={0} | all-to-all | bytes 286720 | tf_op jit(solution)/shard_map/all_to_all | solution.py:147
  288.0 57.5 %all-reduce.4.cloned.1.call-done = f32[144,768]{1,0:T(8,128)} async-done(((f32[144,768]{1,0:T(8,128)}), f32[144,768]{1,0:T(8,128)}) %all-reduce.4.cloned.1.call-update) | async-done | bytes 442384 | tf_op jit(solution)/shard_map/psum | solution.py:151
  345.5 1.4 fusion.32
  347.3 0.9 fusion.84
  348.2 39.1 %reduce-scatter.5.cloned.1.call-done = bf16[192,384]{1,0:T(8,128)(2,1)} async-done(((bf16[1536,384]{1,0:T(8,128)(2,1)}), bf16[192,384]{1,0:T(8,128)(2,1)}) %reduce-scatter.5.cloned.1.call-update) | async-done | bytes 147472 | tf_op jit(solution)/shard_map/reduce_scatter | solution.py:158
  387.2 1.6 convert_bitcast_fusion
  388.9 30.5 %all-gather.10.cloned.1.call-done = bf16[8,40,1792]{2,0,1:T(8,128)(2,1)} async-done(((bf16[8,5,1792]{2,0,1:T(8,128)(2,1)}), bf16[8,40,1792]{2,0,1:T(8,128)(2,1)}) %all-gather.10.cloned.1.call-update) | async-done | bytes 1146896 | tf_op jit(solution)/shard_map/all_gather | solution.py:150
  419.4 1.4 copy.157
  423.3 4.7 %collective-permute-start.2 = (f32[1,64,144]{1,2,0:T(8,128)S(1)}, f32[1,64,144]{1,2,0:T(8,128)S(1)}, u32[]{:S(2)}, u32[]{:S(2)}) collective-permute-start(f32[1,64,144]{1,2,0:T(8,128)S(1)} %get-tuple-element.45), channel_id=1, source_target_pairs={{0,8},{8,16},{16,24},{24,32},{32,40},{40,48},{48,56},{56,64},{64,7... | collective-permute-start | bytes 110600 | tf_op jit(solution)/shard_map/ppermute | solution.py:27
  427.9 1.9 collective-permute-start.3
  429.9 0.8 fusion.15
  430.8 4.6 %collective-permute-done.3 = f32[1,64,144]{1,2,0:T(8,128)S(1)} collective-permute-done((f32[1,64,144]{1,2,0:T(8,128)S(1)}, f32[1,64,144]{1,2,0:T(8,128)S(1)}, u32[]{:S(2)}, u32[]{:S(2)}) %collective-permute-start.3) | collective-permute-done | bytes 36896 | tf_op jit(solution)/shard_map/ppermute | solution.py:29
  (160 shorter events, 19.9 us)
Async XLA Ops:
  7.2 17.0 %copy-start = (bf16[1536,8]{0,1:T(8,128)(2,1)S(1)}, bf16[1536,8]{0,1:T(8,128)(2,1)}, u32[]{:S(2)}) copy-start(bf16[1536,8]{0,1:T(8,128)(2,1)} %param.12) | copy-start | bytes 73732
  7.2 16.0 %copy-start.1 = (bf16[144,1536]{1,0:T(8,128)(2,1)S(1)}, bf16[144,1536]{1,0:T(8,128)(2,1)}, u32[]{:S(2)}) copy-start(bf16[144,1536]{1,0:T(8,128)(2,1)} %param.10) | copy-start | bytes 1327108
  7.2 17.0 %copy-start.18 = (f32[1536]{0:T(1024)S(1)}, f32[1536]{0:T(1024)}, u32[]{:S(2)}) copy-start(f32[1536]{0:T(1024)} %param.11) | copy-start | bytes 18436
  7.2 100.4 %all-gather.6.cloned.1.call-start = ((), (), s32[]{:S(2)}) async-start(), calls=%async_computation.4 | async-start | bytes 1290240 | tf_op jit(solution)/shard_map/all_gather | solution.py:117
  8.0 9.7 %collective-permute-start = (bf16[1,16,64]{2,1,0:T(8,128)(2,1)S(1)}, bf16[1,16,64]{2,1,0:T(8,128)(2,1)S(1)}, u32[]{:S(2)}, u32[]{:S(2)}) collective-permute-start(bf16[1,16,64]{2,1,0:T(8,128)(2,1)S(1)} %get-tuple-element.47), channel_id=1, source_target_pairs={{0,8},{8,16},{16,24},{24,32},{32,40},{40,48},{48,56},{56,64},{64,7... | collective-permute-start | bytes 6152 | tf_op jit(solution)/shard_map/ppermute | solution.py:27
  13.0 6.7 %collective-permute-start.1 = (bf16[1,16,64]{2,1,0:T(8,128)(2,1)S(1)}, bf16[1,16,64]{2,1,0:T(8,128)(2,1)S(1)}, u32[]{:S(2)}, u32[]{:S(2)}) collective-permute-start(bf16[1,16,64]{2,1,0:T(8,128)(2,1)S(1)} %get-tuple-element.48), channel_id=1, source_target_pairs={{8,0},{16,8},{24,16},{32,24},{40,32},{48,40},{56,48},{64,56},{72,6... | collective-permute-start | bytes 6152 | tf_op jit(solution)/shard_map/ppermute | solution.py:29
  16.0 8.5 %copy-start.17 = (s32[128,2]{0,1:T(2,128)S(1)}, s32[128,2]{0,1:T(2,128)}, u32[]{:S(2)}) copy-start(s32[128,2]{0,1:T(2,128)} %param.13) | copy-start | bytes 3076
  17.4 3.1 copy-start.21
  17.4 7.1 %copy-start.19 = (s32[128]{0:T(128)}, s32[128]{0:T(128)S(1)}, u32[]{:S(2)}) copy-start(s32[128]{0:T(128)S(1)} %get-tuple-element.55) | copy-start | bytes 1540
  20.5 4.8 %copy-start.7 = (bf16[128,1536]{1,0:T(8,128)(2,1)S(1)}, bf16[128,1536]{1,0:T(8,128)(2,1)}, u32[]{:S(2)}) copy-start(bf16[128,1536]{1,0:T(8,128)(2,1)} %param.17) | copy-start | bytes 1179652
  23.1 2.2 copy-start.11
  23.5 1.8 copy-start.25
  23.6 2.2 copy-start.2
  25.5 33.1 %copy-start.15 = (bf16[192,384]{1,0:T(8,128)(2,1)S(1)}, bf16[192,384]{1,0:T(8,128)(2,1)}, u32[]{:S(2)}) copy-start(bf16[192,384]{1,0:T(8,128)(2,1)} %param.14) | copy-start | bytes 442372
  25.5 33.1 %copy-start.16 = (bf16[192,384]{1,0:T(8,128)(2,1)S(1)}, bf16[192,384]{1,0:T(8,128)(2,1)}, u32[]{:S(2)}) copy-start(bf16[192,384]{1,0:T(8,128)(2,1)} %param.15) | copy-start | bytes 442372
  58.4 96.8 %all-gather.12.cloned.1.call-start = ((), (), s32[]{:S(2)}) async-start(), calls=%async_computation.10 | async-start | bytes 3981312 | tf_op jit(solution)/shard_map/all_gather | solution.py:68
  60.0 128.5 %all-gather.8.cloned.1.call-start = ((), (), s32[]{:S(2)}) async-start(), calls=%async_computation.5 | async-start | bytes 1327104 | tf_op jit(solution)/shard_map/all_gather | solution.py:70
  60.7 197.3 %reduce-scatter.3.cloned.1.call-start = ((), (), s32[]{:S(2)}) async-start(), calls=%async_computation.6 | async-start | bytes 2064384 | tf_op jit(solution)/shard_map/reduce_scatter | solution.py:144
  110.1 78.5 %copy-start.4 = (bf16[320,1792]{1,0:T(8,128)(2,1)}, bf16[320,1792]{1,0:T(8,128)(2,1)S(1)}, u32[]{:S(2)}) copy-start(bf16[320,1792]{1,0:T(8,128)(2,1)S(1)} %reshape.240) | copy-start | bytes 3440644
  199.6 1.3 copy-start.5
  199.6 1.3 copy-start.10
  199.6 2.4 copy-start.14
  199.6 145.9 %all-reduce.4.cloned.1.call-start = ((), (), s32[]{:S(2)}) async-start(), calls=%async_computation.8 | async-start | bytes 884736 | tf_op jit(solution)/shard_map/psum | solution.py:151
  202.0 185.3 %reduce-scatter.5.cloned.1.call-start = ((), (), s32[]{:S(2)}) async-start(), calls=%async_computation.9 | async-start | bytes 1327104 | tf_op jit(solution)/shard_map/reduce_scatter | solution.py:158
  204.0 83.9 %copy-start.24 = (f32[128]{0:T(128)S(1)}, f32[128]{0:T(128)}, u32[]{:S(2)}) copy-start(f32[128]{0:T(128)} %copy-done.23) | copy-start | bytes 1540
  204.1 215.3 %all-gather.10.cloned.1.call-start = ((), (), s32[]{:S(2)}) async-start(), calls=%async_computation.7 | async-start | bytes 1290240 | tf_op jit(solution)/shard_map/all_gather | solution.py:150
  345.5 1.4 copy-start.6
  388.9 32.0 %copy-start.20 = (s32[128]{0:T(128)S(1)}, s32[128]{0:T(128)}, u32[]{:S(2)}) copy-start(s32[128]{0:T(128)} %copy-done.19) | copy-start | bytes 1540
  388.9 32.2 %copy-start.22 = (s32[128]{0:T(128)S(1)}, s32[128]{0:T(128)}, u32[]{:S(2)}) copy-start(s32[128]{0:T(128)} %copy-done.21) | copy-start | bytes 1540
  421.4 1.1 copy-start.8
  423.3 7.6 %collective-permute-start.2 = (f32[1,64,144]{1,2,0:T(8,128)S(1)}, f32[1,64,144]{1,2,0:T(8,128)S(1)}, u32[]{:S(2)}, u32[]{:S(2)}) collective-permute-start(f32[1,64,144]{1,2,0:T(8,128)S(1)} %get-tuple-element.45), channel_id=1, source_target_pairs={{0,8},{8,16},{16,24},{24,32},{32,40},{40,48},{48,56},{56,64},{64,7... | collective-permute-start | bytes 110600 | tf_op jit(solution)/shard_map/ppermute | solution.py:27
  427.9 7.5 %collective-permute-start.3 = (f32[1,64,144]{1,2,0:T(8,128)S(1)}, f32[1,64,144]{1,2,0:T(8,128)S(1)}, u32[]{:S(2)}, u32[]{:S(2)}) collective-permute-start(f32[1,64,144]{1,2,0:T(8,128)S(1)} %get-tuple-element.46), channel_id=1, source_target_pairs={{8,0},{16,8},{24,16},{32,24},{40,32},{48,40},{56,48},{64,56},{72,6... | collective-permute-start | bytes 110600 | tf_op jit(solution)/shard_map/ppermute | solution.py:29
  (8 other events, 6.8 us)
Sparse Core Ops, SparseCore 0:
  58.6 49.0 all-gather.5
  109.7 45.4 all-gather.11
  157.4 31.1 all-gather.7
  199.7 58.2 reduce-scatter.2
  260.2 85.2 all-reduce.3
  348.2 38.9 reduce-scatter.4
  389.4 29.9 all-gather.9
